TPU v7x, 512 devices: a whole 4x4x16 slice. The times are simulated.
512 devices in a mesh: slab: 16 (over z_lo, core), src: 32 (over y, x, z_hi).
Axes of the slice: x: 4, y: 4, z: 16 (z_hi: 2, z_lo: 8; z = z_hi * 8 + z_lo), core: 2. Of those that a mesh axis runs over, the one named last changes fastest.
Arguments:
- trace_values: bfloat16 [32, 8192, 128], P('src', 'slab'), may hold values from -6 to 6
- trace_owner: int32 [32, 8192, 1], P('src', 'slab'), may hold values from 0 to 15; in each aligned block of 512 rows (0 to 511, 512 to 1023, ..., all dimensions but the last counted through in order) at most 64 rows name the same one
- trace_source: int32 [32, 8192], P('src', 'slab'), may hold values from 0 to 511
- source_fields: bfloat16 [2, 8192, 16384], P(None, 'slab', 'src'), may hold values from -0.03125 to 0.03125
- green_fields: bfloat16 [2, 2048, 16384], P(None, 'slab', 'src'), may hold values from -0.0625 to 0.0625
Outputs:
- gradient: float32 [16384], P('src')
Inputs may be any that keep to these rules, and one draw needn't show every extreme that they name: `trace_owner`: among the traces of one device, no owner is named by more than 64 traces, a bound that some block reaches.
All inputs are finite; a program needn't handle non-finite values.
Results may differ from a plain program's by a relative error of at most 0.0026.
Values may be sent and summed in bfloat16 or wider, within the bound.
A program may use at most 64 MiB of HBM per device.

v0:
```python
import jax
import jax.numpy as jnp
from jax import lax
from jax.sharding import PartitionSpec as P


def on_device(trace_values, trace_owner, trace_source, source_fields, green_fields):
    values = trace_values[0]
    owners = trace_owner[0, :, 0]
    locals_id = trace_source[0]
    trace_count = values.shape[0]
    width = values.shape[1]
    half_width = width // 2
    slab_count = lax.axis_size("slab")
    src_count = lax.axis_size("src")
    sources_here = source_fields.shape[1]
    source_ids = jnp.arange(sources_here, dtype=jnp.int32)
    iota_high = (source_ids // 32).astype(jnp.bfloat16)
    iota_low = (source_ids % 32).astype(jnp.bfloat16)
    capacity = 2 * trace_count // slab_count
    owner_hits = (owners[:, None] == jnp.arange(slab_count, dtype=jnp.int32)[None, :]).astype(
        jnp.int32
    )
    ranks = jnp.sum(jnp.cumsum(owner_hits, axis=0) * owner_hits, axis=1) - 1
    slots = owners * capacity + ranks
    placing = (
        jnp.arange(slab_count * capacity, dtype=jnp.int32)[:, None] == slots[None, :]
    ).astype(jnp.bfloat16)
    sent_values = jnp.dot(placing, values, preferred_element_type=jnp.float32).astype(jnp.bfloat16)
    labels = jnp.stack([locals_id // 32 + 1, locals_id % 32 + 1], axis=1).astype(jnp.bfloat16)
    sent_labels = (jnp.dot(placing, labels, preferred_element_type=jnp.float32) - 1.0).astype(
        jnp.bfloat16
    )
    got_values, got_labels = (
        lax.all_to_all(
            sent_values.reshape(slab_count, capacity, width),
            "slab",
            split_axis=0,
            concat_axis=0,
            tiled=True,
        ),
        lax.all_to_all(
            sent_labels.reshape(slab_count, capacity, 2),
            "slab",
            split_axis=0,
            concat_axis=0,
            tiled=True,
        ),
    )
    flat_labels = got_labels.reshape(-1, 2)
    picks = (
        (iota_high[:, None] == flat_labels[None, :, 0])
        & (iota_low[:, None] == flat_labels[None, :, 1])
    ).astype(jnp.bfloat16)
    assembled = jnp.dot(picks, got_values.reshape(-1, width), preferred_element_type=jnp.float32)
    residual_piece = assembled.astype(jnp.bfloat16)
    residual_rows = lax.all_gather(residual_piece, "src", axis=1, tiled=True)
    split_rows = residual_rows.reshape(sources_here, src_count, 2, half_width)
    res_real = split_rows[:, :, 0, :].reshape(sources_here, src_count * half_width)
    res_imag = split_rows[:, :, 1, :].reshape(sources_here, src_count * half_width)
    piece = lax.all_gather(green_fields, "slab", axis=1, tiled=True)
    adj_real = jnp.dot(res_real, piece[0], preferred_element_type=jnp.float32) + jnp.dot(
        res_imag, piece[1], preferred_element_type=jnp.float32
    )
    adj_imag = jnp.dot(res_real, piece[1], preferred_element_type=jnp.float32) - jnp.dot(
        res_imag, piece[0], preferred_element_type=jnp.float32
    )
    adj_real, adj_imag = (adj_real, adj_imag)
    partial_value = jnp.sum(
        source_fields[0].astype(jnp.float32) * adj_real
        - source_fields[1].astype(jnp.float32) * adj_imag,
        axis=0,
    )
    return lax.psum(partial_value, "slab")


def solution(mesh):
    in_specs = (
        P("src", "slab", None),
        P("src", "slab", None),
        P("src", "slab"),
        P(None, "slab", "src"),
        P(None, "slab", "src"),
    )
    out_specs = P("src")
    return jax.shard_map(
        on_device, mesh=mesh, in_specs=in_specs, out_specs=out_specs, check_vma=False
    )
```

profile of v0, /device:TPU:6, one launch (start us, length us, event | category | flops | bytes accessed | tf_op | source)
XLA Modules:
  0.0 432.0 jit_solution(941762704033851159)
XLA Ops:
  6.5 0.0 copy-start
  6.5 0.7 fusion.31
  7.3 1.1 reduce-window.6
  8.4 0.2 slice_reduce_fusion
  8.7 0.8 fusion.30
  9.4 0.7 add_add_fusion
  10.1 0.7 add_convert_fusion
  10.8 0.5 fusion.21
  11.3 0.1 reshape.180
  11.4 0.6 copy.12
  12.0 12.6 %all-to-all-start = ((bf16[16,64,2]{1,2,0:T(2,128)(2,1)}), bf16[16,64,2]{1,2,0:T(2,128)(2,1)S(1)}, u32[]{:S(2)}, u32[]{:S(2)}) async-start(bf16[16,64,2]{1,2,0:T(2,128)(2,1)} %copy.12), calls=%async_computation | async-start | bytes 16384 | tf_op jit(solution)/shard_map/all_to_all | solution.py:42
  24.6 0.0 copy-done
  24.6 1.2 fusion.16
  25.8 9.2 %all-to-all-done = bf16[16,64,2]{1,2,0:T(2,128)(2,1)S(1)} async-done(((bf16[16,64,2]{1,2,0:T(2,128)(2,1)}), bf16[16,64,2]{1,2,0:T(2,128)(2,1)S(1)}, u32[]{:S(2)}, u32[]{:S(2)}) %all-to-all-start) | async-done | bytes 4128 | tf_op jit(solution)/shard_map/all_to_all | solution.py:42
  35.0 3.5 all-to-all-start.1
  38.5 0.0 all-gather.3.cloned.1.call-start
  38.6 0.1 reshape.181
  38.7 14.7 %all-to-all-done.1 = bf16[16,64,128]{2,1,0:T(8,128)(2,1)S(1)} async-done(((bf16[16,64,128]{2,1,0:T(8,128)(2,1)}), bf16[16,64,128]{2,1,0:T(8,128)(2,1)S(1)}, u32[]{:S(2)}, u32[]{:S(2)}) %all-to-all-start.1) | async-done | bytes 262176 | tf_op jit(solution)/shard_map/all_to_all | solution.py:35
  53.4 1.3 fusion.17
  54.7 0.0 all-gather.3.cloned.1.call-update
  54.7 0.0 all-gather.5.cloned.1.call-start
  54.8 0.7 all-gather.5.cloned.1.call-update
  55.5 208.7 %all-gather.3.cloned.1.call-done = bf16[512,4096]{1,0:T(8,128)(2,1)} async-done(((bf16[512,128]{1,0:T(8,128)(2,1)}), bf16[512,4096]{1,0:T(8,128)(2,1)}) %all-gather.3.cloned.1.call-update) | async-done | bytes 4194320 | tf_op jit(solution)/shard_map/all_gather | solution.py:57
  264.2 6.5 %copy.14 = bf16[512,4096]{0,1:T(8,128)(2,1)} copy(bf16[512,4096]{1,0:T(8,128)(2,1)} %all-gather.3.cloned.1.call-done) | data formatting | bytes 8388608 | tf_op jit(solution)/shard_map/all_gather | solution.py:57
  270.7 4.0 fusion.47
  274.7 89.8 %all-gather.5.cloned.1.call-done = bf16[2,2048,512]{2,1,0:T(8,128)(2,1)} async-done(((bf16[2,128,512]{2,1,0:T(8,128)(2,1)}), bf16[2,2048,512]{2,1,0:T(8,128)(2,1)}) %all-gather.5.cloned.1.call-update) | async-done | bytes 4194320 | tf_op jit(solution)/shard_map/all_gather | solution.py:61
  364.5 0.0 copy-start.1
  364.5 3.0 fusion.7
  367.5 0.0 copy-done.1
  367.5 0.0 copy-start.2
  367.5 0.0 copy-start.3
  367.5 3.0 fusion.6
  370.6 0.0 copy-done.2
  370.6 0.1 copy-done.3
  370.6 1.3 fusion.11
  371.9 1.3 fusion.15
  373.2 51.9 %psum.7 = f32[512]{0:T(512)} all-reduce(f32[512]{0:T(512)S(1)} %fusion.15), channel_id=1, replica_groups=mesh['slab'=16,'src'=32] {'slab'}, use_global_device_ids=true, to_apply=%region_4.5 | all-reduce | flops 512 | bytes 4096 | tf_op jit(solution)/shard_map/psum | solution.py:74
  (6 shorter events, 0.1 us)
Async XLA Ops:
  6.5 18.1 %copy-start = (bf16[1,512,128]{2,1,0:T(8,128)(2,1)S(1)}, bf16[1,512,128]{2,1,0:T(8,128)(2,1)}, u32[]{:S(2)}) copy-start(bf16[1,512,128]{2,1,0:T(8,128)(2,1)} %param.5) | copy-start | bytes 393220
  12.0 23.0 %all-to-all-start = ((bf16[16,64,2]{1,2,0:T(2,128)(2,1)}), bf16[16,64,2]{1,2,0:T(2,128)(2,1)S(1)}, u32[]{:S(2)}, u32[]{:S(2)}) async-start(bf16[16,64,2]{1,2,0:T(2,128)(2,1)} %copy.12), calls=%async_computation | async-start | bytes 16384 | tf_op jit(solution)/shard_map/all_to_all | solution.py:42
  35.0 18.5 %all-to-all-start.1 = ((bf16[16,64,128]{2,1,0:T(8,128)(2,1)}), bf16[16,64,128]{2,1,0:T(8,128)(2,1)S(1)}, u32[]{:S(2)}, u32[]{:S(2)}) async-start(bf16[16,64,128]{2,1,0:T(8,128)(2,1)} %bitcast.6), calls=%async_computation.1 | async-start | bytes 524288 | tf_op jit(solution)/shard_map/all_to_all | solution.py:35
  38.5 225.7 %all-gather.3.cloned.1.call-start = ((), (), s32[]{:S(2)}) async-start(), calls=%async_computation.2 | async-start | bytes 4325376 | tf_op jit(solution)/shard_map/all_gather | solution.py:57
  54.7 309.8 %all-gather.5.cloned.1.call-start = ((), (), s32[]{:S(2)}) async-start(), calls=%async_computation.3 | async-start | bytes 4456448 | tf_op jit(solution)/shard_map/all_gather | solution.py:61
  364.5 3.0 copy-start.1
  367.5 3.0 copy-start.2
  367.5 3.1 copy-start.3
Sparse Core Ops, SparseCore 0:
  54.8 209.3 all-gather.2
  266.3 98.1 all-gather.4
where the time goes:
time: 432 us
  waiting for transfers between devices  323 us (75%)
  blocking collectives  51.9 us (12%)
  starting transfers between devices  16.2 us (4%)
  between operations  13.5 us (3%)
  local copies, waits for them, and re-layouts  11.6 us (3%)
  matrix products  11.5 us (3%)
    all_gather x1, waiting for transfers between devices, on_device(): residual_rows = lax.all_gather(residual_piece, 'src', axis=1, tiled=True)  209 us
    all_gather x1, waiting for transfers between devices, on_device(): piece = lax.all_gather(green_fields, 'slab', axis=1, tiled=True)  89.8 us
    psum x1, blocking collectives, on_device(): return lax.psum(partial_value, 'slab')  51.9 us
    all_to_all x1, waiting for transfers between devices, on_device(): lax.all_to_all(sent_values.reshape(slab_count, capacity, width), 'slab',...  14.7 us
    all_to_all x1, starting transfers between devices, on_device(): lax.all_to_all(sent_labels.reshape(slab_count, capacity, 2), 'slab', spli...  12.6 us
    all_to_all x1, waiting for transfers between devices, on_device(): lax.all_to_all(sent_labels.reshape(slab_count, capacity, 2), 'slab', spli...  9.19 us
  transfers between devices with their start and end apart: 4, of which 4 were waited for; matrix products, arithmetic and copies ran while one was open for 3% of the time, Pallas kernels for 0%

commit v1 on v0

--- a/solution.py
+++ b/solution.py
@@ -54,7 +54,9 @@
     ).astype(jnp.bfloat16)
     assembled = jnp.dot(picks, got_values.reshape(-1, width), preferred_element_type=jnp.float32)
     residual_piece = assembled.astype(jnp.bfloat16)
-    residual_rows = lax.all_gather(residual_piece, "src", axis=1, tiled=True)
+    residual_rows = jnp.concatenate(
+        lax.all_to_all(jnp.stack([residual_piece] * lax.axis_size("src")), "src", 0, 0), axis=1
+    )
     split_rows = residual_rows.reshape(sources_here, src_count, 2, half_width)
     res_real = split_rows[:, :, 0, :].reshape(sources_here, src_count * half_width)
     res_imag = split_rows[:, :, 1, :].reshape(sources_here, src_count * half_width)

time: 432 us -> 367 us (0.85)
  waiting for transfers between devices: 323 us -> 245 us
  starting transfers between devices: 16.2 us -> 29.6 us
    all_gather x1 -> x0, waiting for transfers between devices: 209 us -> none  [on_device(): residual_rows = lax.all_gather(residual_piece, 'src', axis=1, tiled=True)]
    all_to_all x0 -> x1, waiting for transfers between devices: none -> 157 us  [on_device(): lax.all_to_all(jnp.stack([residual_piece] * lax.axis_size('src')), 'src',...]
    all_gather x1, waiting for transfers between devices: 89.8 us -> 63.1 us  [on_device(): piece = lax.all_gather(green_fields, 'slab', axis=1, tiled=True)]
    all_to_all x0 -> x1, starting transfers between devices: none -> 13.4 us  [on_device(): lax.all_to_all(jnp.stack([residual_piece] * lax.axis_size('src')), 'src',...]
    all_gather x1 -> x0, local copies, waits for them, and re-layouts: 6.52 us -> none  [on_device(): residual_rows = lax.all_gather(residual_piece, 'src', axis=1, tiled=True)]
  transfers between devices with their start and end apart: 4 -> 4, of which waited for: 4 -> 4; matrix products, arithmetic and copies ran while one was open for 3% -> 1% of each run, Pallas kernels for 0% -> 0%
where the time goes in v1:
time: 367 us; the launch traced here: 364 us
  waiting for transfers between devices  245 us (67%)
  blocking collectives  53.5 us (15%)
  starting transfers between devices  29.6 us (8%)
  between operations  13.5 us (4%)
  matrix products  10.9 us (3%)
  local copies, waits for them, and re-layouts  7.7 us (2%)
  other arithmetic  4.07 us (1%)
    all_to_all x1, waiting for transfers between devices, on_device(): lax.all_to_all(jnp.stack([residual_piece] * lax.axis_size('src')), 'src',...  157 us
    all_gather x1, waiting for transfers between devices, on_device(): piece = lax.all_gather(green_fields, 'slab', axis=1, tiled=True)  63.1 us
    psum x1, blocking collectives, on_device(): return lax.psum(partial_value, 'slab')  53.5 us
    all_to_all x1, waiting for transfers between devices, on_device(): lax.all_to_all(sent_values.reshape(slab_count, capacity, width), 'slab',...  14.8 us
    all_to_all x1, starting transfers between devices, on_device(): lax.all_to_all(jnp.stack([residual_piece] * lax.axis_size('src')), 'src',...  13.4 us
    all_to_all x1, starting transfers between devices, on_device(): lax.all_to_all(sent_labels.reshape(slab_count, capacity, 2), 'slab', spli...  12.6 us
    all_to_all x1, waiting for transfers between devices, on_device(): lax.all_to_all(sent_labels.reshape(slab_count, capacity, 2), 'slab', spli...  9.19 us
  transfers between devices with their start and end apart: 4, of which 4 were waited for; matrix products, arithmetic and copies ran while one was open for 1% of the time, Pallas kernels for 0%

profile of v1, /device:TPU:6, one launch (start us, length us, event | category | flops | bytes accessed | tf_op | source)
XLA Modules:
  0.0 363.8 jit_solution(10375588930047333384)
XLA Ops:
  6.5 0.0 copy-start
  6.5 0.7 fusion.31
  7.3 1.1 reduce-window.6
  8.4 0.2 slice_reduce_fusion
  8.7 0.8 fusion.30
  9.4 0.7 add_add_fusion
  10.1 0.7 add_convert_fusion
  10.8 0.5 fusion.21
  11.3 0.1 reshape.182
  11.4 0.6 copy.12
  12.0 12.6 %all-to-all-start = ((bf16[16,64,2]{1,2,0:T(2,128)(2,1)}), bf16[16,64,2]{1,2,0:T(2,128)(2,1)S(1)}, u32[]{:S(2)}, u32[]{:S(2)}) async-start(bf16[16,64,2]{1,2,0:T(2,128)(2,1)} %copy.12), calls=%async_computation | async-start | bytes 16384 | tf_op jit(solution)/shard_map/all_to_all | solution.py:42
  24.6 0.0 copy-done
  24.6 1.2 fusion.16
  25.8 9.2 %all-to-all-done = bf16[16,64,2]{1,2,0:T(2,128)(2,1)S(1)} async-done(((bf16[16,64,2]{1,2,0:T(2,128)(2,1)}), bf16[16,64,2]{1,2,0:T(2,128)(2,1)S(1)}, u32[]{:S(2)}, u32[]{:S(2)}) %all-to-all-start) | async-done | bytes 4128 | tf_op jit(solution)/shard_map/all_to_all | solution.py:42
  35.0 3.5 all-to-all-start.1
  38.5 0.1 reshape.183
  38.7 14.8 %all-to-all-done.1 = bf16[16,64,128]{2,1,0:T(8,128)(2,1)S(1)} async-done(((bf16[16,64,128]{2,1,0:T(8,128)(2,1)}), bf16[16,64,128]{2,1,0:T(8,128)(2,1)S(1)}, u32[]{:S(2)}, u32[]{:S(2)}) %all-to-all-start.1) | async-done | bytes 262176 | tf_op jit(solution)/shard_map/all_to_all | solution.py:35
  53.4 0.6 fusion.17
  54.0 0.1 copy.14
  54.2 2.4 stack.6
  56.6 13.4 %all-to-all-start.2 = ((bf16[32,512,128]{1,2,0:T(8,128)(2,1)}), bf16[32,512,128]{1,2,0:T(8,128)(2,1)}, u32[]{:S(2)}, u32[]{:S(2)}) async-start(bf16[32,512,128]{1,2,0:T(8,128)(2,1)} %stack.6), calls=%async_computation.2 | async-start | bytes 8388608 | tf_op jit(solution)/shard_map/all_to_all | solution.py:58
  70.0 0.0 all-gather.2.cloned.1.call-start
  70.0 0.7 all-gather.2.cloned.1.call-update
  70.7 156.9 %all-to-all-done.2 = bf16[32,512,128]{1,2,0:T(8,128)(2,1)} async-done(((bf16[32,512,128]{1,2,0:T(8,128)(2,1)}), bf16[32,512,128]{1,2,0:T(8,128)(2,1)}, u32[]{:S(2)}, u32[]{:S(2)}) %all-to-all-start.2) | async-done | bytes 4194336 | tf_op jit(solution)/shard_map/all_to_all | solution.py:58
  227.6 4.0 %fusion.47 = (bf16[512,32,1,64]{0,3,2,1:T(8,128)(2,1)}, bf16[512,32,1,64]{0,3,2,1:T(8,128)(2,1)S(1)}) fusion(bf16[512,32,2,64]{0,3,2,1:T(8,128)(2,1)} %bitcast.9), kind=kLoop, calls=%fused_computation.67 | loop fusion | bytes 8388608 | tf_op jit(solution)/shard_map/slice | solution.py:62
  231.6 63.1 %all-gather.2.cloned.1.call-done = bf16[2,2048,512]{2,1,0:T(8,128)(2,1)} async-done(((bf16[2,128,512]{2,1,0:T(8,128)(2,1)}), bf16[2,2048,512]{2,1,0:T(8,128)(2,1)}) %all-gather.2.cloned.1.call-update) | async-done | bytes 4194320 | tf_op jit(solution)/shard_map/all_gather | solution.py:63
  294.7 0.0 copy-start.1
  294.7 3.0 fusion.7
  297.7 0.0 copy-done.1
  297.7 0.0 copy-start.2
  297.8 0.0 copy-start.3
  297.8 3.0 fusion.6
  300.8 0.0 copy-done.2
  300.8 0.1 copy-done.3
  300.9 1.3 fusion.11
  302.1 1.3 fusion.15
  303.5 53.5 %psum.7 = f32[512]{0:T(512)} all-reduce(f32[512]{0:T(512)S(1)} %fusion.15), channel_id=1, replica_groups=mesh['slab'=16,'src'=32] {'slab'}, use_global_device_ids=true, to_apply=%region_4.5 | all-reduce | flops 512 | bytes 4096 | tf_op jit(solution)/shard_map/psum | solution.py:76
  (6 shorter events, 0.1 us)
Async XLA Ops:
  6.5 18.1 %copy-start = (bf16[1,512,128]{2,1,0:T(8,128)(2,1)S(1)}, bf16[1,512,128]{2,1,0:T(8,128)(2,1)}, u32[]{:S(2)}) copy-start(bf16[1,512,128]{2,1,0:T(8,128)(2,1)} %param.5) | copy-start | bytes 393220
  12.0 23.0 %all-to-all-start = ((bf16[16,64,2]{1,2,0:T(2,128)(2,1)}), bf16[16,64,2]{1,2,0:T(2,128)(2,1)S(1)}, u32[]{:S(2)}, u32[]{:S(2)}) async-start(bf16[16,64,2]{1,2,0:T(2,128)(2,1)} %copy.12), calls=%async_computation | async-start | bytes 16384 | tf_op jit(solution)/shard_map/all_to_all | solution.py:42
  35.0 18.5 %all-to-all-start.1 = ((bf16[16,64,128]{2,1,0:T(8,128)(2,1)}), bf16[16,64,128]{2,1,0:T(8,128)(2,1)S(1)}, u32[]{:S(2)}, u32[]{:S(2)}) async-start(bf16[16,64,128]{2,1,0:T(8,128)(2,1)} %bitcast.6), calls=%async_computation.1 | async-start | bytes 524288 | tf_op jit(solution)/shard_map/all_to_all | solution.py:35
  56.6 171.0 %all-to-all-start.2 = ((bf16[32,512,128]{1,2,0:T(8,128)(2,1)}), bf16[32,512,128]{1,2,0:T(8,128)(2,1)}, u32[]{:S(2)}, u32[]{:S(2)}) async-start(bf16[32,512,128]{1,2,0:T(8,128)(2,1)} %stack.6), calls=%async_computation.2 | async-start | bytes 8388608 | tf_op jit(solution)/shard_map/all_to_all | solution.py:58
  70.0 224.7 %all-gather.2.cloned.1.call-start = ((), (), s32[]{:S(2)}) async-start(), calls=%async_computation.3 | async-start | bytes 4456448 | tf_op jit(solution)/shard_map/all_gather | solution.py:63
  294.7 3.0 copy-start.1
  297.7 3.0 copy-start.2
  297.8 3.1 copy-start.3
Sparse Core Ops, SparseCore 0:
  72.9 221.7 all-gather.1

commit v2 on v0

--- a/solution.py
+++ b/solution.py
@@ -71,7 +71,7 @@
         - source_fields[1].astype(jnp.float32) * adj_imag,
         axis=0,
     )
-    return lax.psum(partial_value, "slab")
+    return jnp.sum(lax.all_gather(partial_value, "slab"), axis=0)
 
 
 def solution(mesh):

time: 432 us -> 410 us (0.949)
  blocking collectives: 51.9 us -> 27.7 us
    psum x1 -> x0, blocking collectives: 51.9 us -> none  [on_device(): return lax.psum(partial_value, 'slab')]
    all_gather x0 -> x1, blocking collectives: none -> 27.7 us  [on_device(): return jnp.sum(lax.all_gather(partial_value, 'slab'), axis=0)]
where the time goes in v2:
time: 410 us; the launch traced here: 408 us
  waiting for transfers between devices  323 us (79%)
  blocking collectives  27.7 us (7%)
  starting transfers between devices  16.2 us (4%)
  between operations  13.5 us (3%)
  local copies, waits for them, and re-layouts  11.6 us (3%)
  matrix products  11.5 us (3%)
  other arithmetic  4.69 us (1%)
    all_gather x1, waiting for transfers between devices, on_device(): residual_rows = lax.all_gather(residual_piece, 'src', axis=1, tiled=True)  209 us
    all_gather x1, waiting for transfers between devices, on_device(): piece = lax.all_gather(green_fields, 'slab', axis=1, tiled=True)  89.8 us
    all_gather x1, blocking collectives, on_device(): return jnp.sum(lax.all_gather(partial_value, 'slab'), axis=0)  27.7 us
    all_to_all x1, waiting for transfers between devices, on_device(): lax.all_to_all(sent_values.reshape(slab_count, capacity, width), 'slab',...  14.7 us
    all_to_all x1, starting transfers between devices, on_device(): lax.all_to_all(sent_labels.reshape(slab_count, capacity, 2), 'slab', spli...  12.6 us
    all_to_all x1, waiting for transfers between devices, on_device(): lax.all_to_all(sent_labels.reshape(slab_count, capacity, 2), 'slab', spli...  9.19 us
  transfers between devices with their start and end apart: 4, of which 4 were waited for; matrix products, arithmetic and copies ran while one was open for 3% of the time, Pallas kernels for 0%

profile of v2, /device:TPU:6, one launch (start us, length us, event | category | flops | bytes accessed | tf_op | source)
XLA Modules:
  0.0 408.4 jit_solution(1975520161173682005)
XLA Ops:
  6.5 0.0 copy-start
  6.5 0.7 fusion.31
  7.3 1.1 reduce-window.6
  8.4 0.2 slice_reduce_fusion
  8.7 0.8 fusion.30
  9.4 0.7 add_add_fusion
  10.1 0.7 add_convert_fusion
  10.8 0.5 fusion.21
  11.3 0.1 reshape.180
  11.4 0.6 copy.12
  12.0 12.6 %all-to-all-start = ((bf16[16,64,2]{1,2,0:T(2,128)(2,1)}), bf16[16,64,2]{1,2,0:T(2,128)(2,1)S(1)}, u32[]{:S(2)}, u32[]{:S(2)}) async-start(bf16[16,64,2]{1,2,0:T(2,128)(2,1)} %copy.12), calls=%async_computation | async-start | bytes 16384 | tf_op jit(solution)/shard_map/all_to_all | solution.py:42
  24.6 0.0 copy-done
  24.6 1.2 fusion.16
  25.8 9.2 %all-to-all-done = bf16[16,64,2]{1,2,0:T(2,128)(2,1)S(1)} async-done(((bf16[16,64,2]{1,2,0:T(2,128)(2,1)}), bf16[16,64,2]{1,2,0:T(2,128)(2,1)S(1)}, u32[]{:S(2)}, u32[]{:S(2)}) %all-to-all-start) | async-done | bytes 4128 | tf_op jit(solution)/shard_map/all_to_all | solution.py:42
  35.0 3.5 all-to-all-start.1
  38.5 0.0 all-gather.5.cloned.1.call-start
  38.6 0.1 reshape.181
  38.7 14.7 %all-to-all-done.1 = bf16[16,64,128]{2,1,0:T(8,128)(2,1)S(1)} async-done(((bf16[16,64,128]{2,1,0:T(8,128)(2,1)}), bf16[16,64,128]{2,1,0:T(8,128)(2,1)S(1)}, u32[]{:S(2)}, u32[]{:S(2)}) %all-to-all-start.1) | async-done | bytes 262176 | tf_op jit(solution)/shard_map/all_to_all | solution.py:35
  53.4 1.3 fusion.17
  54.7 0.0 all-gather.5.cloned.1.call-update
  54.7 0.0 all-gather.7.cloned.1.call-start
  54.8 0.7 all-gather.7.cloned.1.call-update
  55.5 208.7 %all-gather.5.cloned.1.call-done = bf16[512,4096]{1,0:T(8,128)(2,1)} async-done(((bf16[512,128]{1,0:T(8,128)(2,1)}), bf16[512,4096]{1,0:T(8,128)(2,1)}) %all-gather.5.cloned.1.call-update) | async-done | bytes 4194320 | tf_op jit(solution)/shard_map/all_gather | solution.py:57
  264.2 6.5 %copy.14 = bf16[512,4096]{0,1:T(8,128)(2,1)} copy(bf16[512,4096]{1,0:T(8,128)(2,1)} %all-gather.5.cloned.1.call-done) | data formatting | bytes 8388608 | tf_op jit(solution)/shard_map/all_gather | solution.py:57
  270.7 4.0 fusion.47
  274.7 89.8 %all-gather.7.cloned.1.call-done = bf16[2,2048,512]{2,1,0:T(8,128)(2,1)} async-done(((bf16[2,128,512]{2,1,0:T(8,128)(2,1)}), bf16[2,2048,512]{2,1,0:T(8,128)(2,1)}) %all-gather.7.cloned.1.call-update) | async-done | bytes 4194320 | tf_op jit(solution)/shard_map/all_gather | solution.py:61
  364.5 0.0 copy-start.1
  364.5 3.0 fusion.7
  367.5 0.0 copy-done.1
  367.5 0.0 copy-start.2
  367.5 0.0 copy-start.3
  367.5 3.0 fusion.6
  370.6 0.0 copy-done.2
  370.6 0.1 copy-done.3
  370.6 1.3 fusion.11
  371.9 1.3 fusion.15
  373.3 27.7 %all-gather.1 = f32[16,1,512]{2,1,0:T(1,128)S(1)} all-gather(f32[1,1,512]{2,1,0:T(1,128)S(1)} %bitcast.84), channel_id=2, replica_groups=mesh['slab'=16,'src'=32] {'slab'}, dimensions={0}, use_global_device_ids=true | all-gather | bytes 34816 | tf_op jit(solution)/shard_map/all_gather | solution.py:74
  400.9 0.6 reduce_sum.29
  (6 shorter events, 0.1 us)
Async XLA Ops:
  6.5 18.1 %copy-start = (bf16[1,512,128]{2,1,0:T(8,128)(2,1)S(1)}, bf16[1,512,128]{2,1,0:T(8,128)(2,1)}, u32[]{:S(2)}) copy-start(bf16[1,512,128]{2,1,0:T(8,128)(2,1)} %param.5) | copy-start | bytes 393220
  12.0 23.0 %all-to-all-start = ((bf16[16,64,2]{1,2,0:T(2,128)(2,1)}), bf16[16,64,2]{1,2,0:T(2,128)(2,1)S(1)}, u32[]{:S(2)}, u32[]{:S(2)}) async-start(bf16[16,64,2]{1,2,0:T(2,128)(2,1)} %copy.12), calls=%async_computation | async-start | bytes 16384 | tf_op jit(solution)/shard_map/all_to_all | solution.py:42
  35.0 18.5 %all-to-all-start.1 = ((bf16[16,64,128]{2,1,0:T(8,128)(2,1)}), bf16[16,64,128]{2,1,0:T(8,128)(2,1)S(1)}, u32[]{:S(2)}, u32[]{:S(2)}) async-start(bf16[16,64,128]{2,1,0:T(8,128)(2,1)} %bitcast.6), calls=%async_computation.1 | async-start | bytes 524288 | tf_op jit(solution)/shard_map/all_to_all | solution.py:35
  38.5 225.7 %all-gather.5.cloned.1.call-start = ((), (), s32[]{:S(2)}) async-start(), calls=%async_computation.2 | async-start | bytes 4325376 | tf_op jit(solution)/shard_map/all_gather | solution.py:57
  54.7 309.8 %all-gather.7.cloned.1.call-start = ((), (), s32[]{:S(2)}) async-start(), calls=%async_computation.3 | async-start | bytes 4456448 | tf_op jit(solution)/shard_map/all_gather | solution.py:61
  364.5 3.0 copy-start.1
  367.5 3.0 copy-start.2
  367.5 3.1 copy-start.3
Sparse Core Ops, SparseCore 0:
  54.8 209.3 all-gather.4
  266.3 98.1 all-gather.6
